TPU v7x, 128 devices: a whole 4x4x4 slice. The times are simulated.
128 devices in a mesh: seq: 16 (over x_lo, y, core), heads: 8 (over z, x_hi).
Axes of the slice: x: 4 (x_hi: 2, x_lo: 2; x = x_hi * 2 + x_lo), y: 4, z: 4, core: 2. Of those that a mesh axis runs over, the one named last changes fastest.
Arguments:
- hidden_in: bfloat16 [4096, 8192], P('seq', 'heads'), may hold values from -6 to 6
- queries: bfloat16 [4096, 8192], P('seq', 'heads'), as said below
- image_kv: bfloat16 [16, 2, 6528, 1024], P('seq', None, None, 'heads'), as said below
- out_weight: bfloat16 [8192, 8192], P('seq', 'heads'), may hold values from -0.0625 to 0.0625
- gate: float32 [1], replicated, may hold values from 0.4 to 1.2
- tile_counts: int32 [16], replicated, may hold values from 1 to 4, as said below
- owners: int32 [256], replicated, may hold values from 0 to 15, as said below
- starts: int32 [256], replicated, may hold values from 0 to 3, as said below
- norm_gain: float32 [8192], P('heads'), may hold values from 0.1 to 1.9
- norm_grad: bfloat16 [4096, 8192], P('seq', 'heads'), may hold values from -6 to 6
- stream_grad: bfloat16 [4096, 8192], P('seq', 'heads'), may hold values from -6 to 6
Outputs:
- hidden_out: bfloat16 [4096, 8192], P('seq', 'heads')
- stream_in_grad: float32 [4096, 8192], P('seq', 'heads')
Inputs may be any that keep to these rules, and one draw needn't show every extreme that they name: `tile_counts`: tiles of each image; some image has 4 tiles in every draw. `owners`: the image (named by the seq index that owns it) that a block of 16 text rows attends to; of the 16 blocks of one seq index at most 2 name the same image, and in every draw some image is named by exactly 2 blocks of every seq index. `starts`: the first tile a block sees, below the tile count of the block's image; in every draw some block starts at tile 0 and some at tile 4 - 1. `image_kv`: keys and values are real-valued. real-valued queries.
All inputs are finite; a program needn't handle non-finite values.
Results may differ from a plain program's by a relative error of at most 0.007.
Values may be sent and summed in bfloat16 or wider, within the bound.
No kernel may reach another device: no remote copies, remote signals or barrier semaphores. Data moves between devices by JAX's collectives and lax.ppermute only.
A program may use at most 128 MiB of HBM per device.

v0:
```python
import math
import jax
import jax.numpy as jnp
from jax import lax
from jax.sharding import PartitionSpec as P

D = 8192
HEAD_DIM = 128
TILE_TOK = 1601
BLOCKS_DEV = 16
CAP = 2
BLK = 16
EPS = 1e-05


def head_scores(query_head, key_block, scale):
    return (
        lax.dot_general(
            query_head, key_block, (((1,), (1,)), ((), ())), preferred_element_type=jnp.float32
        )
        * scale
    )


def local(
    hidden_in,
    queries,
    image_kv,
    out_weight,
    gate,
    tile_counts,
    owners,
    starts,
    norm_gain,
    norm_grad,
    stream_grad,
):
    seq_count = lax.axis_size("seq")
    here = lax.axis_index("seq")
    tok_rows, q_width = queries.shape
    q_heads = q_width // HEAD_DIM
    slot_count = seq_count * CAP
    scale = 1.0 / math.sqrt(HEAD_DIM)
    owner_table = owners.reshape(seq_count, BLOCKS_DEV)
    start_table = starts.reshape(seq_count, BLOCKS_DEV)
    my_owner = lax.dynamic_index_in_dim(owner_table, here, 0, keepdims=False)
    block_ids = jnp.arange(BLOCKS_DEV)
    same = my_owner[:, None] == my_owner[None, :]
    earlier = block_ids[None, :] < block_ids[:, None]
    my_rank = jnp.sum(jnp.logical_and(same, earlier).astype(jnp.int32), axis=1)
    my_slot = my_owner * CAP + my_rank
    placing = (my_slot[:, None] == jnp.arange(slot_count)[None, :]).astype(jnp.bfloat16)
    q_blocks = queries.reshape(BLOCKS_DEV, BLK, q_width)
    outgoing = jnp.einsum(
        "bs,brc->src", placing, q_blocks, preferred_element_type=jnp.float32
    ).astype(jnp.bfloat16)
    outgoing = outgoing.reshape(seq_count, CAP, BLK, q_width)
    arriving = owner_table == here
    arrive_rank = jnp.cumsum(arriving.astype(jnp.int32), axis=1) - 1
    slot_hit = jnp.logical_and(
        arriving[:, :, None], arrive_rank[:, :, None] == jnp.arange(CAP)[None, None, :]
    )
    slot_start = jnp.sum(jnp.where(slot_hit, start_table[:, :, None], 0), axis=1)
    tile_here = lax.dynamic_index_in_dim(tile_counts, here, 0, keepdims=False)
    key_end = tile_here * TILE_TOK
    keys_here = image_kv[0, 0]
    values_here = image_kv[0, 1]
    received = lax.all_to_all(outgoing, "seq", split_axis=0, concat_axis=0, tiled=True)
    flat = received.reshape(-1, q_width)
    row_first = jnp.broadcast_to(slot_start[:, :, None], received.shape[:3]).reshape(-1) * TILE_TOK

    def one_head(head):
        query_head = lax.dynamic_slice_in_dim(flat, head * HEAD_DIM, HEAD_DIM, 1)
        spot = jnp.arange(keys_here.shape[0])
        seen = jnp.logical_and(spot[None, :] >= row_first[:, None], spot[None, :] < key_end)
        scores = jnp.where(seen, head_scores(query_head, keys_here, scale), -jnp.inf)
        highest = jnp.max(scores, axis=1, keepdims=True)
        probs = jnp.exp(scores - highest)
        total = jnp.sum(probs, axis=1, keepdims=True)
        mixed = jnp.dot(probs.astype(jnp.bfloat16), values_here, preferred_element_type=jnp.float32)
        return (mixed / total).astype(jnp.bfloat16)

    heads_out = lax.map(one_head, jnp.arange(q_heads))
    merged = jnp.moveaxis(heads_out, 0, 1).reshape(received.shape)
    returned = lax.all_to_all(merged, "seq", split_axis=0, concat_axis=0, tiled=True)
    context = jnp.einsum(
        "bs,src->brc",
        placing,
        returned.reshape(slot_count, BLK, q_width),
        preferred_element_type=jnp.float32,
    )
    context = context.astype(jnp.bfloat16).reshape(tok_rows, q_width)
    full_context = lax.all_gather(context, "heads", axis=1, tiled=True)
    branch = jnp.dot(
        full_context,
        lax.all_gather(out_weight, "seq", axis=0, tiled=True),
        preferred_element_type=jnp.float32,
    )
    hidden_out = (hidden_in.astype(jnp.float32) + jnp.tanh(gate[0]) * branch).astype(jnp.bfloat16)
    hidden = hidden_out.astype(jnp.float32)
    scaled = norm_gain[None, :] * norm_grad.astype(jnp.float32)
    squares, product = lax.psum(
        (jnp.sum(hidden * hidden, axis=1), jnp.sum(hidden * scaled, axis=1)), "heads"
    )
    inverse = lax.rsqrt(squares / D + EPS)[:, None]
    project = (product / D)[:, None]
    stream_in_grad = (
        stream_grad.astype(jnp.float32) + inverse * scaled - inverse**3 * project * hidden
    )
    return (hidden_out, stream_in_grad)


def solution(mesh):
    placed = (
        P("seq", "heads"),
        P("seq", "heads"),
        P("seq", None, None, "heads"),
        P("seq", "heads"),
        P(),
        P(),
        P(),
        P(),
        P("heads"),
        P("seq", "heads"),
        P("seq", "heads"),
    )
    return jax.shard_map(
        local,
        mesh=mesh,
        in_specs=placed,
        out_specs=(P("seq", "heads"), P("seq", "heads")),
        check_vma=False,
    )
```

profile of v0, /device:TPU:0, one launch (start us, length us, event | category | flops | bytes accessed | tf_op | source)
XLA Modules:
  0.0 361.5 jit_solution(7062695272086445816)
XLA Ops:
  11.2 5.7 %all-to-all-start = ((bf16[16,2,16,1024]{3,1,2,0:T(2,128)(2,1)}), bf16[16,2,16,1024]{3,1,2,0:T(2,128)(2,1)}, u32[]{:S(2)}, u32[]{:S(2)}) async-start(bf16[16,2,16,1024]{3,1,2,0:T(2,128)(2,1)} %copy.36), calls=%async_computation | async-start | bytes 2097152 | tf_op jit(solution)/shard_map/all_to_all | solution.py:68
  18.6 3.4 slice_bitcast_fusion
  21.9 11.6 %all-to-all-done = bf16[16,2,16,1024]{3,1,2,0:T(2,128)(2,1)} async-done(((bf16[16,2,16,1024]{3,1,2,0:T(2,128)(2,1)}), bf16[16,2,16,1024]{3,1,2,0:T(2,128)(2,1)}, u32[]{:S(2)}, u32[]{:S(2)}) %all-to-all-start) | async-done | bytes 1048608 | tf_op jit(solution)/shard_map/all_to_all | solution.py:68
  33.5 2.5 copy.37
  36.0 95.0 %while.11 = (s32[]{:T(128)}, bf16[8,512,128]{2,1,0:T(8,128)(2,1)}, s32[]{:T(128)}, s32[8]{0:T(128)S(1)}, bf16[512,1024]{1,0:T(8,128)(2,1)}, /*index=5*/bf16[6528...) while((s32[]{:T(128)}, bf16[8,512,128]{2,1,0:T(8,128)(2,1)}, ...), condition=%wide.region_6.7_spmd.clone, body=%wide.region_3.6_spmd.clone.sunk | while | flops 1741493632 | bytes 43744824 | solution.py:83
  37.5 5.6 %fusion.52 = (f32[512]{0:T(512)S(1)}, f32[512,6528]{1,0:T(8,128)S(1)}) fusion(bf16[6528,128]{1,0:T(8,128)(2,1)} %get-tuple-element.183, bf16[512,1024]{1,0:T(8,128)(2,1)} %get-tuple-element.182, s32[]{:T(128)S(6)} %select_n.24, pred[6528]{0:T(1024)(128)(4,1)S(1)} %iota_compare_fusion.6, s32[512]{0:T(512)S(1)} %mul.129), kind=kOutput, calls=%fused_computation.51.clone.1 | convolution fusion | flops 872349184 | bytes 15182212 | tf_op jit(solution)/shard_map/while/body/eval_jaxpr/dot_general | solution.py:18
  43.1 2.1 fusion.53
  45.2 2.7 fusion.54
  49.3 5.6 %fusion.52 = (f32[512]{0:T(512)S(1)}, f32[512,6528]{1,0:T(8,128)S(1)}) fusion(bf16[6528,128]{1,0:T(8,128)(2,1)} %get-tuple-element.183, bf16[512,1024]{1,0:T(8,128)(2,1)} %get-tuple-element.182, s32[]{:T(128)S(6)} %select_n.24, pred[6528]{0:T(1024)(128)(4,1)S(1)} %iota_compare_fusion.6, s32[512]{0:T(512)S(1)} %mul.129), kind=kOutput, calls=%fused_computation.51.clone.1 | convolution fusion | flops 872349184 | bytes 15182212 | tf_op jit(solution)/shard_map/while/body/eval_jaxpr/dot_general | solution.py:18
  54.9 2.1 fusion.53
  57.0 2.7 fusion.54
  61.2 5.6 %fusion.52 = (f32[512]{0:T(512)S(1)}, f32[512,6528]{1,0:T(8,128)S(1)}) fusion(bf16[6528,128]{1,0:T(8,128)(2,1)} %get-tuple-element.183, bf16[512,1024]{1,0:T(8,128)(2,1)} %get-tuple-element.182, s32[]{:T(128)S(6)} %select_n.24, pred[6528]{0:T(1024)(128)(4,1)S(1)} %iota_compare_fusion.6, s32[512]{0:T(512)S(1)} %mul.129), kind=kOutput, calls=%fused_computation.51.clone.1 | convolution fusion | flops 872349184 | bytes 15182212 | tf_op jit(solution)/shard_map/while/body/eval_jaxpr/dot_general | solution.py:18
  66.8 2.1 fusion.53
  68.9 2.7 fusion.54
  73.1 5.6 %fusion.52 = (f32[512]{0:T(512)S(1)}, f32[512,6528]{1,0:T(8,128)S(1)}) fusion(bf16[6528,128]{1,0:T(8,128)(2,1)} %get-tuple-element.183, bf16[512,1024]{1,0:T(8,128)(2,1)} %get-tuple-element.182, s32[]{:T(128)S(6)} %select_n.24, pred[6528]{0:T(1024)(128)(4,1)S(1)} %iota_compare_fusion.6, s32[512]{0:T(512)S(1)} %mul.129), kind=kOutput, calls=%fused_computation.51.clone.1 | convolution fusion | flops 872349184 | bytes 15182212 | tf_op jit(solution)/shard_map/while/body/eval_jaxpr/dot_general | solution.py:18
  78.7 2.1 fusion.53
  80.8 2.7 fusion.54
  84.9 5.6 %fusion.52 = (f32[512]{0:T(512)S(1)}, f32[512,6528]{1,0:T(8,128)S(1)}) fusion(bf16[6528,128]{1,0:T(8,128)(2,1)} %get-tuple-element.183, bf16[512,1024]{1,0:T(8,128)(2,1)} %get-tuple-element.182, s32[]{:T(128)S(6)} %select_n.24, pred[6528]{0:T(1024)(128)(4,1)S(1)} %iota_compare_fusion.6, s32[512]{0:T(512)S(1)} %mul.129), kind=kOutput, calls=%fused_computation.51.clone.1 | convolution fusion | flops 872349184 | bytes 15182212 | tf_op jit(solution)/shard_map/while/body/eval_jaxpr/dot_general | solution.py:18
  92.7 2.7 fusion.54
  96.8 5.6 %fusion.52 = (f32[512]{0:T(512)S(1)}, f32[512,6528]{1,0:T(8,128)S(1)}) fusion(bf16[6528,128]{1,0:T(8,128)(2,1)} %get-tuple-element.183, bf16[512,1024]{1,0:T(8,128)(2,1)} %get-tuple-element.182, s32[]{:T(128)S(6)} %select_n.24, pred[6528]{0:T(1024)(128)(4,1)S(1)} %iota_compare_fusion.6, s32[512]{0:T(512)S(1)} %mul.129), kind=kOutput, calls=%fused_computation.51.clone.1 | convolution fusion | flops 872349184 | bytes 15182212 | tf_op jit(solution)/shard_map/while/body/eval_jaxpr/dot_general | solution.py:18
  102.4 2.1 fusion.53
  104.5 2.7 fusion.54
  108.7 5.6 %fusion.52 = (f32[512]{0:T(512)S(1)}, f32[512,6528]{1,0:T(8,128)S(1)}) fusion(bf16[6528,128]{1,0:T(8,128)(2,1)} %get-tuple-element.183, bf16[512,1024]{1,0:T(8,128)(2,1)} %get-tuple-element.182, s32[]{:T(128)S(6)} %select_n.24, pred[6528]{0:T(1024)(128)(4,1)S(1)} %iota_compare_fusion.6, s32[512]{0:T(512)S(1)} %mul.129), kind=kOutput, calls=%fused_computation.51.clone.1 | convolution fusion | flops 872349184 | bytes 15182212 | tf_op jit(solution)/shard_map/while/body/eval_jaxpr/dot_general | solution.py:18
  114.3 2.1 fusion.53
  116.4 2.7 fusion.54
  120.6 5.6 %fusion.52 = (f32[512]{0:T(512)S(1)}, f32[512,6528]{1,0:T(8,128)S(1)}) fusion(bf16[6528,128]{1,0:T(8,128)(2,1)} %get-tuple-element.183, bf16[512,1024]{1,0:T(8,128)(2,1)} %get-tuple-element.182, s32[]{:T(128)S(6)} %select_n.24, pred[6528]{0:T(1024)(128)(4,1)S(1)} %iota_compare_fusion.6, s32[512]{0:T(512)S(1)} %mul.129), kind=kOutput, calls=%fused_computation.51.clone.1 | convolution fusion | flops 872349184 | bytes 15182212 | tf_op jit(solution)/shard_map/while/body/eval_jaxpr/dot_general | solution.py:18
  128.3 2.7 fusion.54
  133.4 19.1 %all_to_all.10 = bf16[16,2,16,1024]{3,2,1,0:T(8,128)(2,1)S(1)} all-to-all(bf16[16,2,16,1024]{3,2,1,0:T(8,128)(2,1)S(1)} %reshape.80), channel_id=1, replica_groups=mesh['seq'=16,'heads'=8] {'seq'}, dimensions={0} | all-to-all | bytes 2097152 | tf_op jit(solution)/shard_map/all_to_all | solution.py:85
  156.3 69.8 %all-gather.3.cloned.1.call-done = bf16[256,8192]{1,0:T(8,128)(2,1)} async-done(((bf16[256,1024]{1,0:T(8,128)(2,1)}), bf16[256,8192]{1,0:T(8,128)(2,1)}) %all-gather.3.cloned.1.call-update) | async-done | bytes 4194320 | tf_op jit(solution)/shard_map/all_gather | solution.py:93
  226.0 91.0 %all-gather.5.cloned.1.call-done = bf16[8192,1024]{1,0:T(8,128)(2,1)} async-done(((bf16[512,1024]{1,0:T(8,128)(2,1)}), bf16[8192,1024]{1,0:T(8,128)(2,1)}) %all-gather.5.cloned.1.call-update) | async-done | bytes 16777232 | tf_op jit(solution)/shard_map/all_gather | solution.py:96
  317.1 11.8 %fusion.24 = (f32[256]{0:T(256)S(1)}, f32[256]{0:T(256)S(1)}, bf16[256,1024]{1,0:T(8,128)(2,1)S(1)}) fusion(bf16[256,1024]{1,0:T(8,128)(2,1)S(1)} %copy-done.1, f32[1024]{0:T(1024)S(1)} %copy-done.4, bf16[256,8192]{1,0:T(8,128)(2,1)} %all-gather.3.cloned.1.call-done, bf16[8192,1024]{1,0:T(8,128)(2,1)} %all-gather.5.cloned.1.call-done, f32[]{:T(128)} %bitcast, ...), kind=kOutput, calls=%fused_computation.26 | convolution fusion | flops 4297850880 | bytes 22550532 | tf_op jit(solution)/shard_map/dot_general | solution.py:94
  328.9 24.4 %all-reduce = (f32[256]{0:T(256)S(1)}, f32[256]{0:T(256)S(1)}) all-reduce(f32[256]{0:T(256)S(1)} %get-tuple-element.73, f32[256]{0:T(256)S(1)} %get-tuple-element.72), channel_id=1, replica_groups=mesh['seq'=16,'heads'=8] {'heads'}, use_global_device_ids=true, to_apply=%region_10.11 | all-reduce | flops 512 | bytes 4096 | tf_op jit(solution)/shard_map/psum | solution.py:102
  (75 shorter events, 22.7 us)
Async XLA Ops:
  7.2 1.1 copy-start
  7.2 10.0 %copy-start.5 = (s32[256]{0:T(256)S(1)}, s32[256]{0:T(256)}, u32[]{:S(2)}) copy-start(s32[256]{0:T(256)} %param.20) | copy-start | bytes 3076
  7.2 10.3 %copy-start.6 = (s32[16]{0:T(128)S(1)}, s32[16]{0:T(128)}, u32[]{:S(2)}) copy-start(s32[16]{0:T(128)} %param.18) | copy-start | bytes 196
  11.2 22.3 %all-to-all-start = ((bf16[16,2,16,1024]{3,1,2,0:T(2,128)(2,1)}), bf16[16,2,16,1024]{3,1,2,0:T(2,128)(2,1)}, u32[]{:S(2)}, u32[]{:S(2)}) async-start(bf16[16,2,16,1024]{3,1,2,0:T(2,128)(2,1)} %copy.36), calls=%async_computation | async-start | bytes 2097152 | tf_op jit(solution)/shard_map/all_to_all | solution.py:68
  16.9 209.1 %all-gather.3.cloned.1.call-start = ((), (), s32[]{:S(2)}) async-start(), calls=%async_computation.2 | async-start | bytes 4718592 | tf_op jit(solution)/shard_map/all_gather | solution.py:93
  131.0 186.1 %copy-start.1 = (bf16[256,1024]{1,0:T(8,128)(2,1)S(1)}, bf16[256,1024]{1,0:T(8,128)(2,1)}, u32[]{:S(2)}) copy-start(bf16[256,1024]{1,0:T(8,128)(2,1)} %param.22) | copy-start | bytes 1572868
  131.0 186.1 %copy-start.4 = (f32[1024]{0:T(1024)S(1)}, f32[1024]{0:T(1024)}, u32[]{:S(2)}) copy-start(f32[1024]{0:T(1024)} %param.21) | copy-start | bytes 12292
  154.8 162.2 %all-gather.5.cloned.1.call-start = ((), (), s32[]{:S(2)}) async-start(), calls=%async_computation.3 | async-start | bytes 17825792 | tf_op jit(solution)/shard_map/all_gather | solution.py:96
  317.1 36.3 %copy-start.2 = (bf16[256,1024]{1,0:T(8,128)(2,1)S(1)}, bf16[256,1024]{1,0:T(8,128)(2,1)}, u32[]{:S(2)}) copy-start(bf16[256,1024]{1,0:T(8,128)(2,1)} %param.23) | copy-start | bytes 1572868
  328.9 25.7 %copy-start.3 = (bf16[256,1024]{1,0:T(8,128)(2,1)}, bf16[256,1024]{1,0:T(8,128)(2,1)S(1)}, u32[]{:S(2)}) copy-start(bf16[256,1024]{1,0:T(8,128)(2,1)S(1)} %get-tuple-element.100) | copy-start | bytes 1572868
Sparse Core Ops, SparseCore 0:
  155.0 71.0 all-gather.2
  227.8 89.2 all-gather.4
where the time goes:
time: 362 us; the launch traced here: 361 us
  waiting for transfers between devices  173 us (48%)
  matrix products  80 us (22%)
  blocking collectives  43.5 us (12%)
  local copies, waits for them, and re-layouts  19.9 us (5%)
  other arithmetic  18.7 us (5%)
  between operations  15.4 us (4%)
  starting transfers between devices  5.93 us (2%)
  loops' own time  5.21 us (1%)
    all_gather x1, waiting for transfers between devices, local(): lax.all_gather(out_weight, 'seq', axis=0, tiled=True)  91 us
    all_gather x1, waiting for transfers between devices, local(): full_context = lax.all_gather(context, 'heads', axis=1, tiled=True)  69.8 us
    dot_general x8, matrix products, head_scores(): lax.dot_general(query_head, key_block, (((1,), (1,)), ((), ())), preferre...  44.9 us
    psum x1, blocking collectives, local(): lax.psum((jnp.sum(hidden * hidden, axis=1), jnp.sum(hidden * scaled, axis...  24.4 us
    dot_general x8, matrix products, one_head(): jnp.dot(probs.astype(jnp.bfloat16), values_here, preferred_element_type=j...  21.5 us
    all_to_all x1, blocking collectives, local(): lax.all_to_all(merged, 'seq', split_axis=0, concat_axis=0, tiled=True)  19.1 us
    reduce_sum x8, other arithmetic, one_head(): total = jnp.sum(probs, axis=1, keepdims=True)  16.8 us
    dot_general x1, matrix products, local(): jnp.dot(full_context, lax.all_gather(out_weight, 'seq', axis=0, tiled=Tru...  11.8 us
  transfers between devices with their start and end apart: 3, of which 3 were waited for; matrix products, arithmetic and copies ran while one was open for 1% of the time, Pallas kernels for 0%

commit v1 on v0

--- a/solution.py
+++ b/solution.py
@@ -90,7 +90,8 @@
         preferred_element_type=jnp.float32,
     )
     context = context.astype(jnp.bfloat16).reshape(tok_rows, q_width)
-    full_context = lax.all_gather(context, "heads", axis=1, tiled=True)
+    pieces = lax.all_gather(context, "heads", axis=0, tiled=False)
+    full_context = jnp.concatenate(pieces, axis=1)
     branch = jnp.dot(
         full_context,
         lax.all_gather(out_weight, "seq", axis=0, tiled=True),

time: 362 us -> 362 us (level)
  waiting for transfers between devices: 173 us -> 166 us
  local copies, waits for them, and re-layouts: 19.9 us -> 26.3 us
    all_gather x1, waiting for transfers between devices: 91 us -> 84.6 us  [local(): lax.all_gather(out_weight, 'seq', axis=0, tiled=True)]
    all_gather x0 -> x1, local copies, waits for them, and re-layouts: none -> 6.45 us  [local(): pieces = lax.all_gather(context, 'heads', axis=0, tiled=False)]
  transfers between devices with their start and end apart: 3 -> 3, of which waited for: 3 -> 3; matrix products, arithmetic and copies ran while one was open for 1% -> 3% of each run, Pallas kernels for 0% -> 0%
where the time goes in v1:
time: 362 us; the launch traced here: 361 us
  waiting for transfers between devices  166 us (46%)
  matrix products  80 us (22%)
  blocking collectives  43.5 us (12%)
  local copies, waits for them, and re-layouts  26.3 us (7%)
  other arithmetic  18.7 us (5%)
  between operations  15.4 us (4%)
  starting transfers between devices  5.93 us (2%)
  loops' own time  5.21 us (1%)
    all_gather x1, waiting for transfers between devices, local(): lax.all_gather(out_weight, 'seq', axis=0, tiled=True)  84.6 us
    all_gather x1, waiting for transfers between devices, local(): pieces = lax.all_gather(context, 'heads', axis=0, tiled=False)  69.8 us
    dot_general x8, matrix products, head_scores(): lax.dot_general(query_head, key_block, (((1,), (1,)), ((), ())), preferre...  44.9 us
    psum x1, blocking collectives, local(): lax.psum((jnp.sum(hidden * hidden, axis=1), jnp.sum(hidden * scaled, axis...  24.4 us
    dot_general x8, matrix products, one_head(): jnp.dot(probs.astype(jnp.bfloat16), values_here, preferred_element_type=j...  21.5 us
    all_to_all x1, blocking collectives, local(): lax.all_to_all(merged, 'seq', split_axis=0, concat_axis=0, tiled=True)  19.1 us
    reduce_sum x8, other arithmetic, one_head(): total = jnp.sum(probs, axis=1, keepdims=True)  16.8 us
    dot_general x1, matrix products, local(): jnp.dot(full_context, lax.all_gather(out_weight, 'seq', axis=0, tiled=Tru...  11.9 us
  transfers between devices with their start and end apart: 3, of which 3 were waited for; matrix products, arithmetic and copies ran while one was open for 3% of the time, Pallas kernels for 0%

profile of v1, /device:TPU:0, one launch (start us, length us, event | category | flops | bytes accessed | tf_op | source)
XLA Modules:
  0.0 361.4 jit_solution(7398622198924341694)
XLA Ops:
  11.2 5.7 %all-to-all-start = ((bf16[16,2,16,1024]{3,1,2,0:T(2,128)(2,1)}), bf16[16,2,16,1024]{3,1,2,0:T(2,128)(2,1)}, u32[]{:S(2)}, u32[]{:S(2)}) async-start(bf16[16,2,16,1024]{3,1,2,0:T(2,128)(2,1)} %copy.39), calls=%async_computation | async-start | bytes 2097152 | tf_op jit(solution)/shard_map/all_to_all | solution.py:68
  18.6 3.4 slice_bitcast_fusion
  21.9 11.6 %all-to-all-done = bf16[16,2,16,1024]{3,1,2,0:T(2,128)(2,1)} async-done(((bf16[16,2,16,1024]{3,1,2,0:T(2,128)(2,1)}), bf16[16,2,16,1024]{3,1,2,0:T(2,128)(2,1)}, u32[]{:S(2)}, u32[]{:S(2)}) %all-to-all-start) | async-done | bytes 1048608 | tf_op jit(solution)/shard_map/all_to_all | solution.py:68
  33.5 2.5 copy.40
  36.0 95.0 %while.11 = (s32[]{:T(128)}, bf16[8,512,128]{2,1,0:T(8,128)(2,1)}, s32[]{:T(128)}, s32[8]{0:T(128)S(1)}, bf16[512,1024]{1,0:T(8,128)(2,1)}, /*index=5*/bf16[6528...) while((s32[]{:T(128)}, bf16[8,512,128]{2,1,0:T(8,128)(2,1)}, ...), condition=%wide.region_6.7_spmd.clone, body=%wide.region_3.6_spmd.clone.sunk | while | flops 1741493632 | bytes 43744824 | solution.py:83
  37.5 5.6 %fusion.52 = (f32[512]{0:T(512)S(1)}, f32[512,6528]{1,0:T(8,128)S(1)}) fusion(bf16[6528,128]{1,0:T(8,128)(2,1)} %get-tuple-element.183, bf16[512,1024]{1,0:T(8,128)(2,1)} %get-tuple-element.182, s32[]{:T(128)S(6)} %select_n.24, pred[6528]{0:T(1024)(128)(4,1)S(1)} %iota_compare_fusion.6, s32[512]{0:T(512)S(1)} %mul.129), kind=kOutput, calls=%fused_computation.51.clone.1 | convolution fusion | flops 872349184 | bytes 15182212 | tf_op jit(solution)/shard_map/while/body/eval_jaxpr/dot_general | solution.py:18
  43.1 2.1 fusion.53
  45.2 2.7 fusion.54
  49.3 5.6 %fusion.52 = (f32[512]{0:T(512)S(1)}, f32[512,6528]{1,0:T(8,128)S(1)}) fusion(bf16[6528,128]{1,0:T(8,128)(2,1)} %get-tuple-element.183, bf16[512,1024]{1,0:T(8,128)(2,1)} %get-tuple-element.182, s32[]{:T(128)S(6)} %select_n.24, pred[6528]{0:T(1024)(128)(4,1)S(1)} %iota_compare_fusion.6, s32[512]{0:T(512)S(1)} %mul.129), kind=kOutput, calls=%fused_computation.51.clone.1 | convolution fusion | flops 872349184 | bytes 15182212 | tf_op jit(solution)/shard_map/while/body/eval_jaxpr/dot_general | solution.py:18
  54.9 2.1 fusion.53
  57.0 2.7 fusion.54
  61.2 5.6 %fusion.52 = (f32[512]{0:T(512)S(1)}, f32[512,6528]{1,0:T(8,128)S(1)}) fusion(bf16[6528,128]{1,0:T(8,128)(2,1)} %get-tuple-element.183, bf16[512,1024]{1,0:T(8,128)(2,1)} %get-tuple-element.182, s32[]{:T(128)S(6)} %select_n.24, pred[6528]{0:T(1024)(128)(4,1)S(1)} %iota_compare_fusion.6, s32[512]{0:T(512)S(1)} %mul.129), kind=kOutput, calls=%fused_computation.51.clone.1 | convolution fusion | flops 872349184 | bytes 15182212 | tf_op jit(solution)/shard_map/while/body/eval_jaxpr/dot_general | solution.py:18
  66.8 2.1 fusion.53
  68.9 2.7 fusion.54
  73.1 5.6 %fusion.52 = (f32[512]{0:T(512)S(1)}, f32[512,6528]{1,0:T(8,128)S(1)}) fusion(bf16[6528,128]{1,0:T(8,128)(2,1)} %get-tuple-element.183, bf16[512,1024]{1,0:T(8,128)(2,1)} %get-tuple-element.182, s32[]{:T(128)S(6)} %select_n.24, pred[6528]{0:T(1024)(128)(4,1)S(1)} %iota_compare_fusion.6, s32[512]{0:T(512)S(1)} %mul.129), kind=kOutput, calls=%fused_computation.51.clone.1 | convolution fusion | flops 872349184 | bytes 15182212 | tf_op jit(solution)/shard_map/while/body/eval_jaxpr/dot_general | solution.py:18
  80.8 2.7 fusion.54
  84.9 5.6 %fusion.52 = (f32[512]{0:T(512)S(1)}, f32[512,6528]{1,0:T(8,128)S(1)}) fusion(bf16[6528,128]{1,0:T(8,128)(2,1)} %get-tuple-element.183, bf16[512,1024]{1,0:T(8,128)(2,1)} %get-tuple-element.182, s32[]{:T(128)S(6)} %select_n.24, pred[6528]{0:T(1024)(128)(4,1)S(1)} %iota_compare_fusion.6, s32[512]{0:T(512)S(1)} %mul.129), kind=kOutput, calls=%fused_computation.51.clone.1 | convolution fusion | flops 872349184 | bytes 15182212 | tf_op jit(solution)/shard_map/while/body/eval_jaxpr/dot_general | solution.py:18
  92.7 2.7 fusion.54
  96.8 5.6 %fusion.52 = (f32[512]{0:T(512)S(1)}, f32[512,6528]{1,0:T(8,128)S(1)}) fusion(bf16[6528,128]{1,0:T(8,128)(2,1)} %get-tuple-element.183, bf16[512,1024]{1,0:T(8,128)(2,1)} %get-tuple-element.182, s32[]{:T(128)S(6)} %select_n.24, pred[6528]{0:T(1024)(128)(4,1)S(1)} %iota_compare_fusion.6, s32[512]{0:T(512)S(1)} %mul.129), kind=kOutput, calls=%fused_computation.51.clone.1 | convolution fusion | flops 872349184 | bytes 15182212 | tf_op jit(solution)/shard_map/while/body/eval_jaxpr/dot_general | solution.py:18
  102.4 2.1 fusion.53
  104.5 2.7 fusion.54
  108.7 5.6 %fusion.52 = (f32[512]{0:T(512)S(1)}, f32[512,6528]{1,0:T(8,128)S(1)}) fusion(bf16[6528,128]{1,0:T(8,128)(2,1)} %get-tuple-element.183, bf16[512,1024]{1,0:T(8,128)(2,1)} %get-tuple-element.182, s32[]{:T(128)S(6)} %select_n.24, pred[6528]{0:T(1024)(128)(4,1)S(1)} %iota_compare_fusion.6, s32[512]{0:T(512)S(1)} %mul.129), kind=kOutput, calls=%fused_computation.51.clone.1 | convolution fusion | flops 872349184 | bytes 15182212 | tf_op jit(solution)/shard_map/while/body/eval_jaxpr/dot_general | solution.py:18
  114.3 2.1 fusion.53
  116.4 2.7 fusion.54
  120.6 5.6 %fusion.52 = (f32[512]{0:T(512)S(1)}, f32[512,6528]{1,0:T(8,128)S(1)}) fusion(bf16[6528,128]{1,0:T(8,128)(2,1)} %get-tuple-element.183, bf16[512,1024]{1,0:T(8,128)(2,1)} %get-tuple-element.182, s32[]{:T(128)S(6)} %select_n.24, pred[6528]{0:T(1024)(128)(4,1)S(1)} %iota_compare_fusion.6, s32[512]{0:T(512)S(1)} %mul.129), kind=kOutput, calls=%fused_computation.51.clone.1 | convolution fusion | flops 872349184 | bytes 15182212 | tf_op jit(solution)/shard_map/while/body/eval_jaxpr/dot_general | solution.py:18
  128.3 2.7 fusion.54
  133.4 19.1 %all_to_all.10 = bf16[16,2,16,1024]{3,2,1,0:T(8,128)(2,1)S(1)} all-to-all(bf16[16,2,16,1024]{3,2,1,0:T(8,128)(2,1)S(1)} %reshape.83), channel_id=1, replica_groups=mesh['seq'=16,'heads'=8] {'seq'}, dimensions={0} | all-to-all | bytes 2097152 | tf_op jit(solution)/shard_map/all_to_all | solution.py:85
  156.2 69.8 %all-gather.3.cloned.1.call-done = bf16[8,256,1024]{2,1,0:T(8,128)(2,1)} async-done(((bf16[1,256,1024]{2,1,0:T(8,128)(2,1)}), bf16[8,256,1024]{2,1,0:T(8,128)(2,1)}) %all-gather.3.cloned.1.call-update) | async-done | bytes 4194320 | tf_op jit(solution)/shard_map/all_gather | solution.py:93
  226.0 6.5 %copy.45 = bf16[8,256,1024]{1,2,0:T(8,128)(2,1)} copy(bf16[8,256,1024]{2,1,0:T(8,128)(2,1)} %all-gather.3.cloned.1.call-done) | data formatting | bytes 8388608 | tf_op jit(solution)/shard_map/all_gather | solution.py:93
  232.4 84.6 %all-gather.5.cloned.1.call-done = bf16[8192,1024]{1,0:T(8,128)(2,1)} async-done(((bf16[512,1024]{1,0:T(8,128)(2,1)}), bf16[8192,1024]{1,0:T(8,128)(2,1)}) %all-gather.5.cloned.1.call-update) | async-done | bytes 16777232 | tf_op jit(solution)/shard_map/all_gather | solution.py:97
  317.0 11.9 %fusion.24 = (f32[256]{0:T(256)S(1)}, f32[256]{0:T(256)S(1)}, bf16[256,1024]{1,0:T(8,128)(2,1)S(1)}) fusion(bf16[256,1024]{1,0:T(8,128)(2,1)S(1)} %copy-done.1, f32[1024]{0:T(1024)S(1)} %copy-done.5, bf16[256,8192]{0,1:T(8,128)(2,1)} %bitcast.42, bf16[8192,1024]{1,0:T(8,128)(2,1)} %all-gather.5.cloned.1.call-done, f32[]{:T(128)} %bitcast, ...), kind=kOutput, calls=%fused_computation.26 | convolution fusion | flops 4297850880 | bytes 22550532 | tf_op jit(solution)/shard_map/dot_general | solution.py:95
  328.9 24.4 %all-reduce = (f32[256]{0:T(256)S(1)}, f32[256]{0:T(256)S(1)}) all-reduce(f32[256]{0:T(256)S(1)} %get-tuple-element.73, f32[256]{0:T(256)S(1)} %get-tuple-element.72), channel_id=1, replica_groups=mesh['seq'=16,'heads'=8] {'heads'}, use_global_device_ids=true, to_apply=%region_10.11 | all-reduce | flops 512 | bytes 4096 | tf_op jit(solution)/shard_map/psum | solution.py:103
  (78 shorter events, 24.8 us)
Async XLA Ops:
  7.2 1.1 copy-start
  7.2 10.0 %copy-start.6 = (s32[256]{0:T(256)S(1)}, s32[256]{0:T(256)}, u32[]{:S(2)}) copy-start(s32[256]{0:T(256)} %param.20) | copy-start | bytes 3076
  7.2 10.3 %copy-start.7 = (s32[16]{0:T(128)S(1)}, s32[16]{0:T(128)}, u32[]{:S(2)}) copy-start(s32[16]{0:T(128)} %param.18) | copy-start | bytes 196
  11.2 22.3 %all-to-all-start = ((bf16[16,2,16,1024]{3,1,2,0:T(2,128)(2,1)}), bf16[16,2,16,1024]{3,1,2,0:T(2,128)(2,1)}, u32[]{:S(2)}, u32[]{:S(2)}) async-start(bf16[16,2,16,1024]{3,1,2,0:T(2,128)(2,1)} %copy.39), calls=%async_computation | async-start | bytes 2097152 | tf_op jit(solution)/shard_map/all_to_all | solution.py:68
  16.9 209.1 %all-gather.3.cloned.1.call-start = ((), (), s32[]{:S(2)}) async-start(), calls=%async_computation.2 | async-start | bytes 4718592 | tf_op jit(solution)/shard_map/all_gather | solution.py:93
  152.4 164.6 %copy-start.1 = (bf16[256,1024]{1,0:T(8,128)(2,1)S(1)}, bf16[256,1024]{1,0:T(8,128)(2,1)}, u32[]{:S(2)}) copy-start(bf16[256,1024]{1,0:T(8,128)(2,1)} %param.22) | copy-start | bytes 1572868
  152.4 164.6 %copy-start.3 = (bf16[256,1024]{1,0:T(8,128)(2,1)S(1)}, bf16[256,1024]{1,0:T(8,128)(2,1)}, u32[]{:S(2)}) copy-start(bf16[256,1024]{1,0:T(8,128)(2,1)} %param.13) | copy-start | bytes 1572868
  152.5 164.6 %copy-start.5 = (f32[1024]{0:T(1024)S(1)}, f32[1024]{0:T(1024)}, u32[]{:S(2)}) copy-start(f32[1024]{0:T(1024)} %param.21) | copy-start | bytes 12292
  154.8 162.2 %all-gather.5.cloned.1.call-start = ((), (), s32[]{:S(2)}) async-start(), calls=%async_computation.3 | async-start | bytes 17825792 | tf_op jit(solution)/shard_map/all_gather | solution.py:97
  317.0 36.3 %copy-start.4 = (bf16[256,1024]{1,0:T(8,128)(2,1)S(1)}, bf16[256,1024]{1,0:T(8,128)(2,1)}, u32[]{:S(2)}) copy-start(bf16[256,1024]{1,0:T(8,128)(2,1)} %param.23) | copy-start | bytes 1572868
  328.9 25.7 %copy-start.2 = (bf16[256,1024]{1,0:T(8,128)(2,1)}, bf16[256,1024]{1,0:T(8,128)(2,1)S(1)}, u32[]{:S(2)}) copy-start(bf16[256,1024]{1,0:T(8,128)(2,1)S(1)} %get-tuple-element.100) | copy-start | bytes 1572868
Sparse Core Ops, SparseCore 0:
  154.9 71.0 all-gather.2
  227.7 89.2 all-gather.4
